TPU v7x, 128 devices: a whole 4x4x4 slice. The times are simulated.
128 devices in a mesh: row: 8 (over z, core), col: 16 (over y, x).
Axes of the slice: x: 4, y: 4, z: 4, core: 2. Of those that a mesh axis runs over, the one named last changes fastest.
Arguments:
- front_entries: float32 [16384, 16384], P(None, ('row', 'col')), as said below
- child_updates: float32 [4096, 128, 128], P(('row', 'col')), may hold values from -1 to 1
- row_maps: int32 [4096, 128], P(('row', 'col')), may hold values from 0 to 127, each once within a row
- col_maps: int32 [4096, 128], P(('row', 'col')), may hold values from 0 to 127, each once within a row
- target_columns: int32 [4096, 1], P(('row', 'col')), may hold values from 0 to 127; in each aligned block of 32 rows (0 to 31, 32 to 63, ...) at most 2 rows name the same one
- row_offsets: int32 [4096, 1], P(('row', 'col')), may hold values from 0 to 127
Outputs:
- factored: float32 [16, 8, 8, 16, 128, 128], P(None, 'row', None, 'col')
Inputs may be any that keep to these rules, and one draw needn't show every extreme that they name: `target_columns`: within the rows of one device (aligned blocks of 32 rows) no block column is named more than 2 times; some device names one block column exactly 2 times. `row_maps`: each row is a permutation of 0 to 127. `col_maps`: each row is a permutation of 0 to 127. `front_entries`: entries off the diagonal lie in [0, 2]; diagonal entries lie between 2.5 and 3.5 times the square root of 16384.
All inputs are finite; a program needn't handle non-finite values.
Results may differ from a plain program's by a relative error of at most 0.0001.
Values sent between devices are 32-bit elements; how exact they have to be, the bound alone decides.
A program may use at most 192 MiB of HBM per device.

v0:
```python
import jax
import jax.numpy as jnp
from jax import lax
from jax.sharding import PartitionSpec as P

SLOTS = 2
PANELS = 2
PRECISE = lax.Precision.HIGHEST


def broadcast(value, axis, source):
    kept = jnp.where(lax.axis_index(axis) == source, value, 0).astype(value.dtype)
    return lax.psum(kept, axis)


def place_tiles(tile_set, row_set, col_set):
    levels = jnp.arange(tile_set.shape[1], dtype=jnp.int32)
    row_onehot = (row_set[:, :, None] == levels).astype(jnp.float32)
    col_onehot = (col_set[:, :, None] == levels).astype(jnp.float32)
    half_done = jnp.einsum("nij,njb->nib", tile_set, col_onehot, precision=PRECISE)
    return jnp.einsum("nia,nib->nab", row_onehot, half_done, precision=PRECISE)


def local(front_entries, child_updates, row_maps, col_maps, target_columns, row_offsets):
    grid_rows = lax.axis_size("row")
    grid_cols = lax.axis_size("col")
    block_count = grid_rows * grid_cols
    tile_edge = child_updates.shape[1]
    held_count = child_updates.shape[0]
    columns = target_columns[:, 0]
    offsets = row_offsets[:, 0]
    target_rows = columns + offsets % (block_count - columns)
    placed = place_tiles(child_updates, row_maps, col_maps)
    serial = jnp.arange(held_count, dtype=jnp.int32)
    earlier = (columns[:, None] == columns[None, :]) & (serial[None, :] < serial[:, None])
    slot_rank = jnp.sum(earlier.astype(jnp.int32), axis=1)
    position = columns * SLOTS + slot_rank
    outgoing = (
        jnp.zeros((block_count * SLOTS, tile_edge, tile_edge), jnp.float32).at[position].set(placed)
    )
    targets = jnp.zeros((block_count * SLOTS,), jnp.int32).at[position].set(target_rows)
    arrived, landing = (
        lax.all_to_all(outgoing, ("row", "col"), split_axis=0, concat_axis=0, tiled=True),
        lax.all_to_all(targets, ("row", "col"), split_axis=0, concat_axis=0, tiled=True),
    )
    own_blocks = front_entries.reshape(block_count, tile_edge, tile_edge)
    column_blocks = own_blocks + jax.ops.segment_sum(arrived, landing, num_segments=block_count)
    grid_tiles = lax.all_to_all(
        column_blocks.reshape(block_count // grid_rows, grid_rows, tile_edge, tile_edge),
        "row",
        split_axis=1,
        concat_axis=1,
        tiled=True,
    )
    my_row = lax.axis_index("row")
    my_col = lax.axis_index("col")
    block_rows = jnp.arange(block_count // grid_rows, dtype=jnp.int32) * grid_rows + my_row
    block_cols = jnp.arange(block_count // grid_cols, dtype=jnp.int32) * grid_cols + my_col
    stride = grid_cols // grid_rows
    for panel_idx in range(PANELS):
        local_row = panel_idx // grid_rows
        prepare_local_col = panel_idx // grid_cols
        pivot_tile = broadcast(
            grid_tiles[local_row, prepare_local_col], "row", panel_idx % grid_rows
        )
        symmetric = jnp.tril(pivot_tile) + jnp.tril(pivot_tile, -1).T
        pivot_factor = jnp.linalg.cholesky(symmetric)
        panel_rows = grid_tiles[:, prepare_local_col].reshape(-1, tile_edge)
        solved = jax.scipy.linalg.solve_triangular(pivot_factor, panel_rows.T, lower=True).T
        solved = solved.reshape(-1, tile_edge, tile_edge)
        lower_part = jnp.where((block_rows > panel_idx)[:, None, None], solved, 0.0)
        prepare_written = jnp.where(
            (block_rows == panel_idx)[:, None, None], pivot_factor[None], lower_part
        )
        prepare_shared = broadcast(lower_part, "col", panel_idx % grid_cols)
        chosen = lax.dynamic_index_in_dim(
            prepare_shared.reshape(block_count // grid_cols, stride, tile_edge, tile_edge),
            my_col // grid_rows,
            1,
            keepdims=False,
        )
        prepare_across = broadcast(chosen, "row", my_col % grid_rows)
        tiles_now = grid_tiles - jnp.einsum(
            "jab,scb->jsac", prepare_shared, prepare_across, precision=PRECISE
        )
        local_col = panel_idx // grid_cols
        fresh = jnp.where(my_col == panel_idx % grid_cols, prepare_written, tiles_now[:, local_col])
        grid_tiles = tiles_now.at[:, local_col].set(fresh)
    row_grid = block_rows[:, None, None, None]
    col_grid = block_cols[None, :, None, None]
    inside = jnp.arange(tile_edge)[:, None] >= jnp.arange(tile_edge)[None, :]
    keep_mask = (row_grid > col_grid) | (row_grid == col_grid) & inside[None, None]
    result = jnp.where(keep_mask, grid_tiles, 0.0)
    return result.reshape(
        block_count // grid_rows, 1, block_count // grid_cols, 1, tile_edge, tile_edge
    )


def solution(mesh):
    return jax.shard_map(
        local,
        mesh=mesh,
        in_specs=(
            P(None, ("row", "col")),
            P(("row", "col"), None, None),
            P(("row", "col"), None),
            P(("row", "col"), None),
            P(("row", "col"), None),
            P(("row", "col"), None),
        ),
        out_specs=P(None, "row", None, "col", None, None),
        check_vma=False,
    )
```

profile of v0, /device:TPU:0, one launch (start us, length us, event | category | flops | bytes accessed | tf_op | source)
XLA Modules:
  0.0 978.0 jit_solution(2281378333469623732)
XLA Ops:
  6.5 6.0 copy.132
  14.3 11.2 %all-to-all-start = ((s32[128,2,1]{1,2,0:T(1,128)}), s32[128,2,1]{1,2,0:T(1,128)S(1)}, u32[]{:S(2)}, u32[]{:S(2)}) async-start(s32[128,2,1]{1,2,0:T(1,128)} %bitcast.5), calls=%async_computation | async-start | bytes 131072 | tf_op jit(solution)/shard_map/all_to_all | solution.py:44
  30.1 7.8 broadcast_in_dim.130
  37.9 5.5 scatter_fusion
  43.4 10.3 %all-to-all-start.1 = ((f32[256,128,128]{2,1,0:T(8,128)}), f32[256,128,128]{2,1,0:T(8,128)}, u32[]{:S(2)}, u32[]{:S(2)}) async-start(f32[256,128,128]{2,1,0:T(8,128)} %scatter_fusion), calls=%async_computation.1 | async-start | bytes 33554432 | tf_op jit(solution)/shard_map/all_to_all | solution.py:43
  55.2 218.6 %all-to-all-done.1 = f32[256,128,128]{2,1,0:T(8,128)} async-done(((f32[256,128,128]{2,1,0:T(8,128)}), f32[256,128,128]{2,1,0:T(8,128)}, u32[]{:S(2)}, u32[]{:S(2)}) %all-to-all-start.1) | async-done | bytes 16777248 | tf_op jit(solution)/shard_map/all_to_all | solution.py:43
  273.8 55.1 %scatter_fusion.1 = f32[128,128,128]{2,1,0:T(8,128)} fusion(f32[128,128,128]{2,1,0:T(8,128)} %bitcast.110, s32[256]{0:T(256)S(1)} %reshape.269, f32[256,128,128]{2,1,0:T(8,128)} %all-to-all-done.1), kind=kCustom, calls=%fused_computation.2 | custom fusion | flops 4194304 | bytes 50332672 | tf_op jit(solution)/shard_map/scatter-add | solution.py:47
  328.9 7.7 copy.86
  336.6 32.8 %all-to-all-start.2 = ((f32[16,8,128,128]{3,2,0,1:T(8,128)}), f32[16,8,128,128]{3,2,0,1:T(8,128)}, u32[]{:S(2)}, u32[]{:S(2)}) async-start(f32[16,8,128,128]{3,2,0,1:T(8,128)} %copy.86), calls=%async_computation.2 | async-start | bytes 16777216 | tf_op jit(solution)/shard_map/all_to_all | solution.py:48
  369.4 94.6 %all-to-all-done.2 = f32[16,8,128,128]{3,2,0,1:T(8,128)} async-done(((f32[16,8,128,128]{3,2,0,1:T(8,128)}), f32[16,8,128,128]{3,2,0,1:T(8,128)}, u32[]{:S(2)}, u32[]{:S(2)}) %all-to-all-start.2) | async-done | bytes 8388640 | tf_op jit(solution)/shard_map/all_to_all | solution.py:48
  467.1 59.4 %all-reduce.7.cloned.1.call-done = f32[128,128]{1,0:T(8,128)} async-done(((f32[128,128]{1,0:T(8,128)}), f32[128,128]{1,0:T(8,128)}) %all-reduce.7.cloned.1.call-update) | async-done | bytes 65552 | tf_op jit(solution)/shard_map/psum | solution.py:13
  528.5 11.7 %cholesky.44 = f32[128,128]{1,0:T(8,128)S(1)} custom-call(f32[128,128]{1,0:T(8,128)S(1)} %fusion.25), custom_call_target="Cholesky" | custom-call | tf_op jit(solution)/shard_map/jit(cholesky)/cholesky | solution.py:67
  541.6 9.8 %custom-call.6 = f32[1,128,128]{1,2,0:T(8,128)S(1)} custom-call(f32[1,128,128]{2,1,0:T(8,128)S(1)} %get-tuple-element.33), custom_call_target="InvertDiagBlocksLowerTriangular" | custom-call | tf_op jit(solution)/shard_map/jit(_solve_triangular)/triangular_solve | solution.py:69
  554.1 86.0 %all-reduce.9.cloned.1.call-done = f32[16,128,128]{2,1,0:T(8,128)} async-done(((f32[16,128,128]{2,1,0:T(8,128)}), f32[16,128,128]{2,1,0:T(8,128)}) %all-reduce.9.cloned.1.call-update) | async-done | bytes 1048592 | tf_op jit(solution)/shard_map/psum | solution.py:13
  642.2 60.8 %all-reduce.11.cloned.1.call-done = f32[8,128,128]{2,1,0:T(8,128)} async-done(((f32[8,128,128]{2,1,0:T(8,128)}), f32[8,128,128]{2,1,0:T(8,128)}) %all-reduce.11.cloned.1.call-update) | async-done | bytes 524304 | tf_op jit(solution)/shard_map/psum | solution.py:13
  703.0 10.0 %bitcast_subtract_fusion.1 = f32[16,8,128,128]{3,2,1,0:T(8,128)S(1)} fusion(f32[16,128,128]{2,1,0:T(8,128)} %all-reduce.9.cloned.1.call-done, f32[8,128,128]{2,1,0:T(8,128)} %all-reduce.11.cloned.1.call-done, f32[16,8,128,128]{3,2,0,1:T(8,128)} %all-to-all-done.2), kind=kOutput, calls=%fused_computation.4 | convolution fusion | flops 3223322624 | bytes 18350080 | tf_op jit(solution)/shard_map/jab,scb->jsac/dot_general | solution.py:83
  713.0 3.4 copy-done.2
  720.4 57.2 %all-reduce.13.cloned.1.call-done = f32[128,128]{1,0:T(8,128)} async-done(((f32[128,128]{1,0:T(8,128)}), f32[128,128]{1,0:T(8,128)}) %all-reduce.13.cloned.1.call-update) | async-done | bytes 65552 | tf_op jit(solution)/shard_map/psum | solution.py:13
  779.5 11.7 %cholesky.55 = f32[128,128]{1,0:T(8,128)S(1)} custom-call(f32[128,128]{1,0:T(8,128)S(1)} %fusion.23), custom_call_target="Cholesky" | custom-call | tf_op jit(solution)/shard_map/jit(cholesky)/cholesky | solution.py:67
  792.7 9.8 %custom-call.7 = f32[1,128,128]{1,2,0:T(8,128)S(1)} custom-call(f32[1,128,128]{2,1,0:T(8,128)S(1)} %get-tuple-element.31), custom_call_target="InvertDiagBlocksLowerTriangular" | custom-call | tf_op jit(solution)/shard_map/jit(_solve_triangular)/triangular_solve | solution.py:69
  808.1 85.7 %all-reduce.15.cloned.1.call-done = f32[16,128,128]{2,1,0:T(8,128)} async-done(((f32[16,128,128]{2,1,0:T(8,128)}), f32[16,128,128]{2,1,0:T(8,128)}) %all-reduce.15.cloned.1.call-update) | async-done | bytes 1048592 | tf_op jit(solution)/shard_map/psum | solution.py:13
  896.8 59.7 %all-reduce.17.cloned.1.call-done = f32[8,128,128]{2,1,0:T(8,128)} async-done(((f32[8,128,128]{2,1,0:T(8,128)}), f32[8,128,128]{2,1,0:T(8,128)}) %all-reduce.17.cloned.1.call-update) | async-done | bytes 524304 | tf_op jit(solution)/shard_map/psum | solution.py:13
  956.5 10.1 %bitcast_subtract_fusion = f32[16,8,128,128]{3,2,1,0:T(8,128)S(1)} fusion(f32[16,8,128,128]{3,2,1,0:T(8,128)} %constant_dynamic-update-slice_fusion, f32[16,128,128]{2,1,0:T(8,128)} %all-reduce.15.cloned.1.call-done, f32[8,128,128]{2,1,0:T(8,128)} %all-reduce.17.cloned.1.call-done), kind=kOutput, calls=%fused_computation.3 | convolution fusion | flops 3223322624 | bytes 18350080 | tf_op jit(solution)/shard_map/jab,scb->jsac/dot_general | solution.py:83
  966.9 4.2 select_bitcast_fusion
  (79 shorter events, 35.0 us)
Async XLA Ops:
  6.5 19.0 %copy-start = (f32[32,128,128]{2,1,0:T(8,128)S(1)}, f32[32,128,128]{2,1,0:T(8,128)}, u32[]{:S(2)}) copy-start(f32[32,128,128]{2,1,0:T(8,128)} %param.14) | copy-start | bytes 6291460
  6.5 6.0 copy-start.5
  6.5 6.2 copy-start.6
  6.5 19.0 %copy-start.3 = (s32[32,128]{1,0:T(8,128)S(1)}, s32[32,128]{1,0:T(8,128)}, u32[]{:S(2)}) copy-start(s32[32,128]{1,0:T(8,128)} %param.16) | copy-start | bytes 49156
  6.5 21.3 %copy-start.4 = (s32[32,128]{1,0:T(8,128)S(1)}, s32[32,128]{1,0:T(8,128)}, u32[]{:S(2)}) copy-start(s32[32,128]{1,0:T(8,128)} %param.15) | copy-start | bytes 49156
  14.3 29.1 %all-to-all-start = ((s32[128,2,1]{1,2,0:T(1,128)}), s32[128,2,1]{1,2,0:T(1,128)S(1)}, u32[]{:S(2)}, u32[]{:S(2)}) async-start(s32[128,2,1]{1,2,0:T(1,128)} %bitcast.5), calls=%async_computation | async-start | bytes 131072 | tf_op jit(solution)/shard_map/all_to_all | solution.py:44
  43.4 230.4 %all-to-all-start.1 = ((f32[256,128,128]{2,1,0:T(8,128)}), f32[256,128,128]{2,1,0:T(8,128)}, u32[]{:S(2)}, u32[]{:S(2)}) async-start(f32[256,128,128]{2,1,0:T(8,128)} %scatter_fusion), calls=%async_computation.1 | async-start | bytes 33554432 | tf_op jit(solution)/shard_map/all_to_all | solution.py:43
  336.6 127.5 %all-to-all-start.2 = ((f32[16,8,128,128]{3,2,0,1:T(8,128)}), f32[16,8,128,128]{3,2,0,1:T(8,128)}, u32[]{:S(2)}, u32[]{:S(2)}) async-start(f32[16,8,128,128]{3,2,0,1:T(8,128)} %copy.86), calls=%async_computation.2 | async-start | bytes 16777216 | tf_op jit(solution)/shard_map/all_to_all | solution.py:48
  369.4 157.2 %all-reduce.7.cloned.1.call-start = ((), (), s32[]{:S(2)}) async-start(), calls=%async_computation.3 | async-start | bytes 131072 | tf_op jit(solution)/shard_map/psum | solution.py:13
  465.6 174.6 %all-reduce.9.cloned.1.call-start = ((), (), s32[]{:S(2)}) async-start(), calls=%async_computation.4 | async-start | bytes 2097152 | tf_op jit(solution)/shard_map/psum | solution.py:13
  554.0 149.0 %all-reduce.11.cloned.1.call-start = ((), (), s32[]{:S(2)}) async-start(), calls=%async_computation.5 | async-start | bytes 1048576 | tf_op jit(solution)/shard_map/psum | solution.py:13
  642.0 135.5 %all-reduce.13.cloned.1.call-start = ((), (), s32[]{:S(2)}) async-start(), calls=%async_computation.6 | async-start | bytes 131072 | tf_op jit(solution)/shard_map/psum | solution.py:13
  713.0 3.4 copy-start.2
  718.3 175.5 %all-reduce.15.cloned.1.call-start = ((), (), s32[]{:S(2)}) async-start(), calls=%async_computation.7 | async-start | bytes 2097152 | tf_op jit(solution)/shard_map/psum | solution.py:13
  807.7 148.8 %all-reduce.17.cloned.1.call-start = ((), (), s32[]{:S(2)}) async-start(), calls=%async_computation.8 | async-start | bytes 1048576 | tf_op jit(solution)/shard_map/psum | solution.py:13
  966.9 4.3 copy-start.1
Sparse Core Ops, SparseCore 0:
  465.7 60.8 all-reduce.6
  554.1 85.9 all-reduce.8
  642.5 60.4 all-reduce.10
  718.4 59.0 all-reduce.12
  807.8 85.9 all-reduce.14
  896.0 60.4 all-reduce.16
where the time goes:
time: 979 us; the launch traced here: 978 us
  waiting for transfers between devices  722 us (74%)
  other arithmetic  119 us (12%)
  starting transfers between devices  55.1 us (6%)
  local copies, waits for them, and re-layouts  39.9 us (4%)
  matrix products  28.1 us (3%)
  between operations  13.9 us (1%)
    psum x6, waiting for transfers between devices, broadcast(): return lax.psum(kept, axis)  409 us
    all_to_all x1, waiting for transfers between devices, local(): lax.all_to_all(outgoing, ('row', 'col'), split_axis=0, concat_axis=0, til...  219 us
    all_to_all x1, waiting for transfers between devices, local(): lax.all_to_all(column_blocks.reshape(block_count // grid_rows, grid_rows,...  94.6 us
    scatter-add x1, other arithmetic, local(): jax.ops.segment_sum(arrived, landing, num_segments=block_count)  55.1 us
    all_to_all x1, starting transfers between devices, local(): lax.all_to_all(column_blocks.reshape(block_count // grid_rows, grid_rows,...  32.8 us
    another operation x6, other arithmetic, local(): pivot_factor = jnp.linalg.cholesky(symmetric)  24.9 us
    another operation x4, other arithmetic, local(): jax.scipy.linalg.solve_triangular(pivot_factor, panel_rows.T, lower=True)  21 us
    dot_general x2, matrix products, local(): jnp.einsum('jab,scb->jsac', prepare_shared, prepare_across, precision=PRE...  20.1 us
  transfers between devices with their start and end apart: 9, of which 8 were waited for; matrix products, arithmetic and copies ran while one was open for 2% of the time, Pallas kernels for 0%

commit v1 on v0

--- a/solution.py
+++ b/solution.py
@@ -10,7 +10,7 @@
 
 def broadcast(value, axis, source):
     kept = jnp.where(lax.axis_index(axis) == source, value, 0).astype(value.dtype)
-    return lax.psum(kept, axis)
+    return jnp.sum(lax.all_gather(kept, axis_name=axis), axis=0)
 
 
 def place_tiles(tile_set, row_set, col_set):

time: 979 us -> 917 us (0.937)
  waiting for transfers between devices: 722 us -> 598 us
  blocking collectives: 0 us -> 26.7 us
  local copies, waits for them, and re-layouts: 39.9 us -> 54.6 us
  other arithmetic: 119 us -> 132 us
    psum x6 -> x0, waiting for transfers between devices: 409 us -> none  [broadcast(): return lax.psum(kept, axis)]
    all_gather x0 -> x4, waiting for transfers between devices: none -> 284 us  [broadcast(): return jnp.sum(lax.all_gather(kept, axis_name=axis), axis=0)]
    all_gather x0 -> x2, blocking collectives: none -> 26.7 us  [broadcast(): return jnp.sum(lax.all_gather(kept, axis_name=axis), axis=0)]
    reduce_sum x0 -> x6, other arithmetic: none -> 20 us  [broadcast(): return jnp.sum(lax.all_gather(kept, axis_name=axis), axis=0)]
  transfers between devices with their start and end apart: 9 -> 7, of which waited for: 8 -> 6; matrix products, arithmetic and copies ran while one was open for 2% -> 2% of each run, Pallas kernels for 0% -> 0%
where the time goes in v1:
time: 917 us; the launch traced here: 907 us
  waiting for transfers between devices  598 us (65%)
  other arithmetic  132 us (14%)
  starting transfers between devices  54.8 us (6%)
  local copies, waits for them, and re-layouts  54.6 us (6%)
  matrix products  27.6 us (3%)
  blocking collectives  26.7 us (3%)
  between operations  13.8 us (2%)
    all_gather x4, waiting for transfers between devices, broadcast(): return jnp.sum(lax.all_gather(kept, axis_name=axis), axis=0)  284 us
    all_to_all x1, waiting for transfers between devices, local(): lax.all_to_all(outgoing, ('row', 'col'), split_axis=0, concat_axis=0, til...  219 us
    all_to_all x1, waiting for transfers between devices, local(): lax.all_to_all(column_blocks.reshape(block_count // grid_rows, grid_rows,...  94.6 us
    scatter-add x1, other arithmetic, local(): jax.ops.segment_sum(arrived, landing, num_segments=block_count)  55.1 us
    all_to_all x1, starting transfers between devices, local(): lax.all_to_all(column_blocks.reshape(block_count // grid_rows, grid_rows,...  32.8 us
    all_gather x2, blocking collectives, broadcast(): return jnp.sum(lax.all_gather(kept, axis_name=axis), axis=0)  26.7 us
    another operation x6, other arithmetic, local(): pivot_factor = jnp.linalg.cholesky(symmetric)  24.9 us
    another operation x4, other arithmetic, local(): jax.scipy.linalg.solve_triangular(pivot_factor, panel_rows.T, lower=True)  21 us
  transfers between devices with their start and end apart: 7, of which 6 were waited for; matrix products, arithmetic and copies ran while one was open for 2% of the time, Pallas kernels for 0%

profile of v1, /device:TPU:0, one launch (start us, length us, event | category | flops | bytes accessed | tf_op | source)
XLA Modules:
  0.0 907.3 jit_solution(10450341239794513907)
XLA Ops:
  6.5 6.0 copy.99
  14.3 11.2 %all-to-all-start = ((s32[128,2,1]{1,2,0:T(1,128)}), s32[128,2,1]{1,2,0:T(1,128)S(1)}, u32[]{:S(2)}, u32[]{:S(2)}) async-start(s32[128,2,1]{1,2,0:T(1,128)} %bitcast.5), calls=%async_computation | async-start | bytes 131072 | tf_op jit(solution)/shard_map/all_to_all | solution.py:44
  30.1 7.8 broadcast_in_dim.130
  37.9 5.5 scatter_fusion
  43.4 10.3 %all-to-all-start.1 = ((f32[256,128,128]{2,1,0:T(8,128)}), f32[256,128,128]{2,1,0:T(8,128)}, u32[]{:S(2)}, u32[]{:S(2)}) async-start(f32[256,128,128]{2,1,0:T(8,128)} %scatter_fusion), calls=%async_computation.1 | async-start | bytes 33554432 | tf_op jit(solution)/shard_map/all_to_all | solution.py:43
  55.2 218.6 %all-to-all-done.1 = f32[256,128,128]{2,1,0:T(8,128)} async-done(((f32[256,128,128]{2,1,0:T(8,128)}), f32[256,128,128]{2,1,0:T(8,128)}, u32[]{:S(2)}, u32[]{:S(2)}) %all-to-all-start.1) | async-done | bytes 16777248 | tf_op jit(solution)/shard_map/all_to_all | solution.py:43
  273.8 55.1 %scatter_fusion.1 = f32[128,128,128]{2,1,0:T(8,128)} fusion(f32[128,128,128]{2,1,0:T(8,128)} %bitcast.108, s32[256]{0:T(256)S(1)} %reshape.335, f32[256,128,128]{2,1,0:T(8,128)} %all-to-all-done.1), kind=kCustom, calls=%fused_computation.2 | custom fusion | flops 4194304 | bytes 50332672 | tf_op jit(solution)/shard_map/scatter-add | solution.py:47
  328.9 7.7 copy.56
  336.6 32.8 %all-to-all-start.2 = ((f32[16,8,128,128]{3,2,0,1:T(8,128)}), f32[16,8,128,128]{3,2,0,1:T(8,128)}, u32[]{:S(2)}, u32[]{:S(2)}) async-start(f32[16,8,128,128]{3,2,0,1:T(8,128)} %copy.56), calls=%async_computation.2 | async-start | bytes 16777216 | tf_op jit(solution)/shard_map/all_to_all | solution.py:48
  369.5 94.6 %all-to-all-done.2 = f32[16,8,128,128]{3,2,0,1:T(8,128)} async-done(((f32[16,8,128,128]{3,2,0,1:T(8,128)}), f32[16,8,128,128]{3,2,0,1:T(8,128)}, u32[]{:S(2)}, u32[]{:S(2)}) %all-to-all-start.2) | async-done | bytes 8388640 | tf_op jit(solution)/shard_map/all_to_all | solution.py:48
  464.9 13.6 %all-gather = f32[8,1,128,128]{3,2,1,0:T(8,128)S(1)} all-gather(f32[1,1,128,128]{3,2,1,0:T(8,128)S(1)} %fusion.19), channel_id=2, replica_groups=mesh['row'=8,'col'=16] {'row'}, dimensions={0}, use_global_device_ids=true | all-gather | bytes 589824 | tf_op jit(solution)/shard_map/all_gather | solution.py:13
  478.8 11.7 %cholesky.44 = f32[128,128]{1,0:T(8,128)S(1)} custom-call(f32[128,128]{1,0:T(8,128)S(1)} %fusion.24), custom_call_target="Cholesky" | custom-call | tf_op jit(solution)/shard_map/jit(cholesky)/cholesky | solution.py:67
  491.9 9.8 %custom-call.6 = f32[1,128,128]{1,2,0:T(8,128)S(1)} custom-call(f32[1,128,128]{2,1,0:T(8,128)S(1)} %get-tuple-element.33), custom_call_target="InvertDiagBlocksLowerTriangular" | custom-call | tf_op jit(solution)/shard_map/jit(_solve_triangular)/triangular_solve | solution.py:69
  505.7 112.3 %all-gather.9.cloned.1.call-done = f32[16,16,128,128]{3,2,1,0:T(8,128)} async-done(((f32[1,16,128,128]{3,2,1,0:T(8,128)}), f32[16,16,128,128]{3,2,1,0:T(8,128)}) %all-gather.9.cloned.1.call-update) | async-done | bytes 16777232 | tf_op jit(solution)/shard_map/all_gather | solution.py:13
  618.0 7.4 reduce_sum.73
  633.5 31.2 %all-gather.13.cloned.1.call-done = f32[64,1,128,128]{3,2,1,0:T(8,128)} async-done(((f32[8,1,128,128]{3,2,1,0:T(8,128)}), f32[64,1,128,128]{3,2,1,0:T(8,128)}) %all-gather.13.cloned.1.call-update) | async-done | bytes 4194320 | tf_op jit(solution)/shard_map/all_gather | solution.py:13
  667.3 9.8 %bitcast_subtract_fusion.1 = f32[16,8,128,128]{3,2,0,1:T(8,128)S(1)} fusion(f32[16,8,128,128]{3,2,0,1:T(8,128)} %all-to-all-done.2, f32[16,128,128]{2,1,0:T(8,128)S(1)} %reduce_sum.73, f32[8,128,128]{2,1,0:T(8,128)S(1)} %bitcast_reduce_fusion.1), kind=kOutput, calls=%fused_computation.4 | convolution fusion | flops 3223322624 | bytes 18350080 | tf_op jit(solution)/shard_map/jab,scb->jsac/dot_general | solution.py:83
  681.7 13.1 %all-gather.2 = f32[8,1,128,128]{3,2,1,0:T(8,128)S(1)} all-gather(f32[1,1,128,128]{3,2,1,0:T(8,128)S(1)} %fusion.18), channel_id=4, replica_groups=mesh['row'=8,'col'=16] {'row'}, dimensions={0}, use_global_device_ids=true | all-gather | bytes 589824 | tf_op jit(solution)/shard_map/all_gather | solution.py:13
  695.1 11.7 %cholesky.55 = f32[128,128]{1,0:T(8,128)S(1)} custom-call(f32[128,128]{1,0:T(8,128)S(1)} %fusion.21), custom_call_target="Cholesky" | custom-call | tf_op jit(solution)/shard_map/jit(cholesky)/cholesky | solution.py:67
  708.3 9.8 %custom-call.7 = f32[1,128,128]{1,2,0:T(8,128)S(1)} custom-call(f32[1,128,128]{2,1,0:T(8,128)S(1)} %get-tuple-element.31), custom_call_target="InvertDiagBlocksLowerTriangular" | custom-call | tf_op jit(solution)/shard_map/jit(_solve_triangular)/triangular_solve | solution.py:69
  725.2 110.5 %all-gather.11.cloned.1.call-done = f32[16,16,128,128]{3,2,1,0:T(8,128)} async-done(((f32[1,16,128,128]{3,2,1,0:T(8,128)}), f32[16,16,128,128]{3,2,1,0:T(8,128)}) %all-gather.11.cloned.1.call-update) | async-done | bytes 16777232 | tf_op jit(solution)/shard_map/all_gather | solution.py:13
  835.7 7.5 reduce_sum.77
  852.2 30.3 %all-gather.15.cloned.1.call-done = f32[64,1,128,128]{3,2,1,0:T(8,128)} async-done(((f32[8,1,128,128]{3,2,1,0:T(8,128)}), f32[64,1,128,128]{3,2,1,0:T(8,128)}) %all-gather.15.cloned.1.call-update) | async-done | bytes 4194320 | tf_op jit(solution)/shard_map/all_gather | solution.py:13
  885.1 9.8 %bitcast_subtract_fusion = f32[16,8,128,128]{3,2,0,1:T(8,128)S(1)} fusion(f32[16,8,128,128]{3,2,0,1:T(8,128)} %constant_dynamic-update-slice_fusion, f32[16,128,128]{2,1,0:T(8,128)S(1)} %reduce_sum.77, f32[8,128,128]{2,1,0:T(8,128)S(1)} %bitcast_reduce_fusion), kind=kOutput, calls=%fused_computation.3 | convolution fusion | flops 3223322624 | bytes 18350080 | tf_op jit(solution)/shard_map/jab,scb->jsac/dot_general | solution.py:83
  (91 shorter events, 55.3 us)
Async XLA Ops:
  6.5 19.0 %copy-start = (f32[32,128,128]{2,1,0:T(8,128)S(1)}, f32[32,128,128]{2,1,0:T(8,128)}, u32[]{:S(2)}) copy-start(f32[32,128,128]{2,1,0:T(8,128)} %param.14) | copy-start | bytes 6291460
  6.5 6.0 copy-start.7
  6.5 6.2 copy-start.8
  6.5 19.0 %copy-start.5 = (s32[32,128]{1,0:T(8,128)S(1)}, s32[32,128]{1,0:T(8,128)}, u32[]{:S(2)}) copy-start(s32[32,128]{1,0:T(8,128)} %param.16) | copy-start | bytes 49156
  6.5 21.3 %copy-start.6 = (s32[32,128]{1,0:T(8,128)S(1)}, s32[32,128]{1,0:T(8,128)}, u32[]{:S(2)}) copy-start(s32[32,128]{1,0:T(8,128)} %param.15) | copy-start | bytes 49156
  14.3 29.1 %all-to-all-start = ((s32[128,2,1]{1,2,0:T(1,128)}), s32[128,2,1]{1,2,0:T(1,128)S(1)}, u32[]{:S(2)}, u32[]{:S(2)}) async-start(s32[128,2,1]{1,2,0:T(1,128)} %bitcast.5), calls=%async_computation | async-start | bytes 131072 | tf_op jit(solution)/shard_map/all_to_all | solution.py:44
  43.4 230.4 %all-to-all-start.1 = ((f32[256,128,128]{2,1,0:T(8,128)}), f32[256,128,128]{2,1,0:T(8,128)}, u32[]{:S(2)}, u32[]{:S(2)}) async-start(f32[256,128,128]{2,1,0:T(8,128)} %scatter_fusion), calls=%async_computation.1 | async-start | bytes 33554432 | tf_op jit(solution)/shard_map/all_to_all | solution.py:43
  336.6 127.5 %all-to-all-start.2 = ((f32[16,8,128,128]{3,2,0,1:T(8,128)}), f32[16,8,128,128]{3,2,0,1:T(8,128)}, u32[]{:S(2)}, u32[]{:S(2)}) async-start(f32[16,8,128,128]{3,2,0,1:T(8,128)} %copy.56), calls=%async_computation.2 | async-start | bytes 16777216 | tf_op jit(solution)/shard_map/all_to_all | solution.py:48
  369.4 248.6 %all-gather.9.cloned.1.call-start = ((), (), s32[]{:S(2)}) async-start(), calls=%async_computation.3 | async-start | bytes 17825792 | tf_op jit(solution)/shard_map/all_gather | solution.py:13
  505.6 159.2 %all-gather.13.cloned.1.call-start = ((), (), s32[]{:S(2)}) async-start(), calls=%async_computation.5 | async-start | bytes 4718592 | tf_op jit(solution)/shard_map/all_gather | solution.py:13
  633.1 202.6 %all-gather.11.cloned.1.call-start = ((), (), s32[]{:S(2)}) async-start(), calls=%async_computation.4 | async-start | bytes 17825792 | tf_op jit(solution)/shard_map/all_gather | solution.py:13
  677.1 3.4 copy-start.2
  681.7 43.5 %copy-start.3 = (f32[16,1,128,128]{3,2,0,1:T(8,128)}, f32[16,1,128,128]{3,2,0,1:T(8,128)S(1)}, u32[]{:S(2)}) copy-start(f32[16,1,128,128]{3,2,0,1:T(8,128)S(1)} %get-tuple-element.36) | copy-start | bytes 3145732
  724.9 157.7 %all-gather.15.cloned.1.call-start = ((), (), s32[]{:S(2)}) async-start(), calls=%async_computation.6 | async-start | bytes 4718592 | tf_op jit(solution)/shard_map/all_gather | solution.py:13
  835.7 15.5 %copy-start.4 = (f32[16,1,128,128]{3,2,0,1:T(8,128)S(1)}, f32[16,1,128,128]{3,2,0,1:T(8,128)}, u32[]{:S(2)}) copy-start(f32[16,1,128,128]{3,2,0,1:T(8,128)} %copy-done.3) | copy-start | bytes 3145732
  895.2 5.3 copy-start.1
Sparse Core Ops, SparseCore 0:
  505.7 112.2 all-gather.8
  633.2 31.4 all-gather.12
  725.0 110.6 all-gather.10
  851.0 31.4 all-gather.14
